TPU v7x, 32 devices: a whole 2x2x4 slice. The times are simulated.
32 devices in a mesh: strip: 8 (over z, x), col: 4 (over y, core).
Axes of the slice: x: 2, y: 2, z: 4, core: 2. Of those that a mesh axis runs over, the one named last changes fastest.
Arguments:
- net_box: int32 [32768, 4], P(('strip', 'col')), may hold values from 0 to 1023, as said below
- net_weight: float32 [32768], P(('strip', 'col')), may hold values from 0.5 to 2
- pin_bin: int32 [32768, 4, 2], P(('strip', 'col')), may hold values from 0 to 1023, as said below
- conv_first: bfloat16 [3, 3, 32, 3], replicated, may hold values from -1.25 to 1.25
- bias_first: float32 [32], replicated, may hold values from -3 to 3
- conv_second: bfloat16 [3, 3, 32, 32], replicated, may hold values from -0.375 to 0.375
- bias_second: float32 [32], replicated, may hold values from -3 to 3
- cotangent: bfloat16 [512, 32, 1024], P('col', None, 'strip'), may hold values from -6 to 6
Outputs:
- congestion: bfloat16 [512, 32, 1024], P('col', None, 'strip')
- net_grad: float32 [32768], P(('strip', 'col'))
Inputs may be any that keep to these rules, and one draw needn't show every extreme that they name: `net_box`: box n = (x0, x1, y0, y1) has x0 <= x1 < x0 + 16 and y0 <= y1 < y0 + 16; y0 lies in rows s * 128 to (s + 1) * 128 - 1, where s = n // 4096 is the strip whose devices hold net n. Some box is 16 bins tall and wide. `pin_bin`: every pin of net n lies in net n's box.
All inputs are finite; a program needn't handle non-finite values.
Results may differ from a plain program's by a relative error of at most 0.0054.
Values may be sent and summed in bfloat16 or wider, within the bound.
No kernel may reach another device: no remote copies, remote signals or barrier semaphores. Data moves between devices by JAX's collectives and lax.ppermute only.
A program may use at most 192 MiB of HBM per device.

v0:
```python
import math
import jax
import jax.numpy as jnp
from jax import lax
from jax.sharding import PartitionSpec as P


def from_behind(x, axis, by):
    size = lax.axis_size(axis)
    pairs = [(i, i + by) for i in range(size) if 0 <= i + by < size]
    return lax.ppermute(x, axis, pairs)


def with_halo(block, sides, width):
    for axis, dim in sides:
        count = lax.axis_size(axis)
        forward = [(i, i + 1) for i in range(count - 1)]
        backward = [(target, source) for source, target in forward]
        low = lax.ppermute(
            lax.slice_in_dim(block, block.shape[dim] - width, None, axis=dim), axis, forward
        )
        high = lax.ppermute(lax.slice_in_dim(block, 0, width, axis=dim), axis, backward)
        block = jnp.concatenate([low, block, high], axis=dim)
    return block


def silu_slope(pre_act):
    sigmoid = jax.nn.sigmoid(pre_act)
    return sigmoid * (1.0 + pre_act * (1.0 - sigmoid))


def conv_valid(padded, weights, out_cols, out_rows):
    summed = None
    for shift_row in range(3):
        for shift_col in range(3):
            window = padded[shift_col : shift_col + out_cols, :, shift_row : shift_row + out_rows]
            product = jnp.einsum(
                "oi,xiy->xoy",
                weights[shift_row, shift_col],
                window,
                preferred_element_type=jnp.float32,
            )
            summed = product if summed is None else summed + product
    return summed


def conv_back(padded, weights, out_cols, out_rows):
    summed = None
    for shift_row in range(3):
        for shift_col in range(3):
            window = padded[
                2 - shift_col : 2 - shift_col + out_cols,
                :,
                2 - shift_row : 2 - shift_row + out_rows,
            ]
            product = jnp.einsum(
                "oi,xoy->xiy",
                weights[shift_row, shift_col],
                window,
                preferred_element_type=jnp.float32,
            )
            summed = product if summed is None else summed + product
    return summed


def strip_factors(box_rows, weights, pin_list, first_row, span):
    row_ids = first_row + jnp.arange(2 * span, dtype=jnp.int32)
    top_row = box_rows[:, 2]
    bottom_row = box_rows[:, 3]
    inside = (top_row[:, None] <= row_ids[None, :]) & (row_ids[None, :] <= bottom_row[:, None])
    box_height = (bottom_row - top_row + 1).astype(jnp.float32)
    box_width = (box_rows[:, 1] - box_rows[:, 0] + 1).astype(jnp.float32)
    values = jnp.stack([weights / box_height, weights / box_width], axis=1).astype(jnp.bfloat16)
    row_factor = inside.astype(jnp.bfloat16).reshape(-1, 2, 1, span) * values[:, None, :, None]
    pin_rows = pin_list[:, :, 0].reshape(-1)
    pin_factor = (pin_rows[:, None] == row_ids[None, :]).astype(jnp.bfloat16).reshape(-1, 2, span)
    return (row_factor, pin_list[:, :, 1].reshape(-1), pin_factor)


def column_block(col_ids, left_col, right_col, row_factor, pin_col, pin_factor):
    net_cols = (
        (left_col[:, None] <= col_ids[None, :]) & (col_ids[None, :] <= right_col[:, None])
    ).astype(jnp.bfloat16)
    pin_cols = (pin_col[:, None] == col_ids[None, :]).astype(jnp.bfloat16)
    demand = jnp.einsum("nk,nhcr->khcr", net_cols, row_factor, preferred_element_type=jnp.float32)
    density = jnp.einsum("pk,phr->khr", pin_cols, pin_factor, preferred_element_type=jnp.float32)
    return jnp.concatenate([demand, density[:, :, None, :]], axis=2)


def shards(
    net_box, net_weight, pin_bin, conv_first, bias_first, conv_second, bias_second, cotangent
):
    tile_cols = cotangent.shape[0]
    span = cotangent.shape[2]
    net_total = net_box.shape[0]
    strip_index = lax.axis_index("strip")
    col_index = lax.axis_index("col")
    all_rows = span * lax.axis_size("strip")
    all_cols = tile_cols * lax.axis_size("col")
    first_row = strip_index * span
    pin_width = pin_bin.shape[1]
    packed = jnp.concatenate(
        [
            net_box.astype(jnp.float32),
            pin_bin.reshape(net_total, 2 * pin_width).astype(jnp.float32),
            net_weight[:, None],
        ],
        axis=1,
    )
    own_cols = col_index * tile_cols + jnp.arange(tile_cols, dtype=jnp.int32)
    start_terms = jnp.zeros((tile_cols, 2, 3, span), jnp.float32)
    shard_piece = lax.all_gather(packed, "col", axis=0, tiled=True)
    piece_rows = shard_piece.shape[0]
    block_size = math.gcd(piece_rows, 1024)
    grouped = shard_piece.reshape(piece_rows // block_size, block_size, shard_piece.shape[1])

    def one_group(summed, net_group):
        box_rows = net_group[:, :4].astype(jnp.int32)
        pin_list = (
            net_group[:, 4 : 4 + 2 * pin_width].reshape(block_size, pin_width, 2).astype(jnp.int32)
        )
        weights = net_group[:, 4 + 2 * pin_width]
        row_factor, pin_col, pin_factor = strip_factors(
            box_rows, weights, pin_list, first_row, span
        )
        return (
            summed
            + column_block(
                own_cols, box_rows[:, 0], box_rows[:, 1], row_factor, pin_col, pin_factor
            ),
            None,
        )

    summed, unused = lax.scan(one_group, start_terms, grouped)
    spilled = from_behind(summed[:, 1].astype(jnp.bfloat16), "strip", 1).astype(jnp.float32)
    features = (summed[:, 0] + spilled).astype(jnp.bfloat16)
    stacked = jnp.concatenate([features, cotangent], axis=1)
    padded = with_halo(stacked, (("strip", 2), ("col", 0)), 2)
    in_channels = features.shape[1]
    col_ids = col_index * tile_cols - 1 + jnp.arange(tile_cols + 2, dtype=jnp.int32)
    row_ids = first_row - 1 + jnp.arange(span + 2, dtype=jnp.int32)
    inside = ((col_ids >= 0) & (col_ids < all_cols))[:, None, None] & (
        (row_ids >= 0) & (row_ids < all_rows)
    )[None, None, :]
    pre_act = (
        conv_valid(padded[:, :in_channels], conv_first, tile_cols + 2, span + 2)
        + bias_first[None, :, None]
    )
    hidden = jnp.where(inside, jax.nn.silu(pre_act), 0.0).astype(jnp.bfloat16)
    congestion = (
        conv_valid(hidden, conv_second, tile_cols, span) + bias_second[None, :, None]
    ).astype(jnp.bfloat16)
    back_hidden = conv_back(padded[:, in_channels:], conv_second, tile_cols + 2, span + 2)
    back_pre = jnp.where(inside, back_hidden * silu_slope(pre_act), 0.0).astype(jnp.bfloat16)
    back_maps = conv_back(back_pre, conv_first[:, :, :, :2], tile_cols, span).astype(jnp.bfloat16)
    from_below = from_behind(back_maps, "strip", -1)
    both_halves = jnp.stack([back_maps, from_below], axis=1).reshape(tile_cols, 4 * span)
    left_col = net_box[:, 0]
    right_col = net_box[:, 1]
    shard_piece = lax.all_gather(both_halves, "col", axis=0, tiled=True)
    piece_cols = jnp.arange(shard_piece.shape[0], dtype=jnp.int32)
    net_cols = (
        (left_col[:, None] <= piece_cols[None, :]) & (piece_cols[None, :] <= right_col[:, None])
    ).astype(jnp.bfloat16)
    column_sums = jnp.dot(net_cols, shard_piece, preferred_element_type=jnp.float32)
    column_sums = column_sums.reshape(net_total, 2, 2, span)
    net_rows = first_row + jnp.arange(2 * span, dtype=jnp.int32)
    in_rows = (
        (
            (net_box[:, 2][:, None] <= net_rows[None, :])
            & (net_rows[None, :] <= net_box[:, 3][:, None])
        )
        .astype(jnp.float32)
        .reshape(net_total, 2, span)
    )
    box_height = (net_box[:, 3] - net_box[:, 2] + 1).astype(jnp.float32)
    box_width = (right_col - left_col + 1).astype(jnp.float32)
    per_row = (
        column_sums[:, :, 0] / box_height[:, None, None]
        + column_sums[:, :, 1] / box_width[:, None, None]
    )
    net_grad = jnp.sum(in_rows * per_row, axis=(1, 2))
    return (congestion, net_grad)


def solution(mesh):
    placed = (
        P(("strip", "col"), None),
        P(("strip", "col")),
        P(("strip", "col"), None, None),
        P(),
        P(),
        P(),
        P(),
        P("col", None, "strip"),
    )
    return jax.shard_map(
        shards,
        mesh=mesh,
        in_specs=placed,
        out_specs=(P("col", None, "strip"), P(("strip", "col"))),
        check_vma=False,
    )
```

profile of v0, /device:TPU:19, one launch (start us, length us, event | category | flops | bytes accessed | tf_op | source)
XLA Modules:
  0.0 179.9 jit_solution(665664036078959381)
XLA Ops:
  2.9 6.3 %all_gather.6 = f32[4096,13]{0,1:T(8,128)S(1)} all-gather(f32[1024,13]{0,1:T(8,128)S(1)} %pad_maximum_fusion.10), channel_id=1, replica_groups=mesh['strip'=8,'col'=4] {'col'}, dimensions={0}, use_global_device_ids=true | all-gather | bytes 266240 | tf_op jit(solution)/shard_map/all_gather | solution.py:112
  9.4 13.7 %while.11 = (s32[]{:T(128)}, f32[128,2,3,128]{3,0,2,1:T(8,128)S(1)}, f32[4,1024,13]{1,0,2:T(4,128)S(1)}, s32[]{:T(128)}, s32[]{:T(128)}, /*index=5*/s32[]{:T(128)}, s32[]{:T(128)}) while((s32[]{:T(128)}, f32[128,2,3,128]{3,0,2,1:T(8,128)S(1)}, f32[4,1024,13]{1,0,2:T(4,128)S(1)}, s32[]{:T(128)}, s32[]{:T(128)}, ...), condition=%wide.region_1.2_spmd.clone, body=%wide.region_0.1_spmd.clone.sunk | while | flops 408091520 | bytes 3318379 | solution.py:134
  23.3 3.2 %collective-permute-start = (bf16[128,3,128]{0,2,1:T(8,128)(2,1)S(1)}, bf16[128,3,128]{0,2,1:T(8,128)(2,1)S(1)}, u32[]{:S(2)}, u32[]{:S(2)}) collective-permute-start(bf16[128,3,128]{0,2,1:T(8,128)(2,1)S(1)} %fusion.144), channel_id=1, source_target_pairs={{0,4},{4,8},{8,12},{12,16},{16,20},{20,24},{24,28},{1,5},{5,9},{9,... | collective-permute-start | bytes 294920 | tf_op jit(solution)/shard_map/ppermute | solution.py:11
  29.5 3.1 %collective-permute-start.2 = (bf16[128,35,2]{0,2,1:T(2,128)(2,1)S(1)}, bf16[128,35,2]{0,2,1:T(2,128)(2,1)S(1)}, u32[]{:S(2)}, u32[]{:S(2)}) collective-permute-start(bf16[128,35,2]{0,2,1:T(2,128)(2,1)S(1)} %get-tuple-element.87), channel_id=1, source_target_pairs={{4,0},{8,4},{12,8},{16,12},{20,16},{24,20},{28,24},{5,1},{9,5},{13... | collective-permute-start | bytes 53768 | tf_op jit(solution)/shard_map/ppermute | solution.py:22
  32.6 3.1 %collective-permute-start.1 = (bf16[128,35,2]{0,2,1:T(2,128)(2,1)S(1)}, bf16[128,35,2]{0,2,1:T(2,128)(2,1)S(1)}, u32[]{:S(2)}, u32[]{:S(2)}) collective-permute-start(bf16[128,35,2]{0,2,1:T(2,128)(2,1)S(1)} %get-tuple-element.86), channel_id=1, source_target_pairs={{0,4},{4,8},{8,12},{12,16},{16,20},{20,24},{24,28},{1,5},{5,9},{9,... | collective-permute-start | bytes 53768 | tf_op jit(solution)/shard_map/ppermute | solution.py:19
  38.7 3.6 %copy.58 = bf16[128,35,132]{2,1,0:T(8,128)(2,1)S(1)} copy(bf16[128,35,132]{0,2,1:T(8,128)(2,1)} %pad_maximum_fusion.8) | data formatting | bytes 2365440 | tf_op jit(solution)/shard_map/concatenate | solution.py:23
  42.3 5.4 %collective-permute-start.3 = (bf16[2,35,132]{2,1,0:T(8,128)(2,1)S(1)}, bf16[2,35,132]{2,1,0:T(8,128)(2,1)S(1)}, u32[]{:S(2)}, u32[]{:S(2)}) collective-permute-start(bf16[2,35,132]{2,1,0:T(8,128)(2,1)S(1)} %get-tuple-element.84), channel_id=1, source_target_pairs={{0,1},{1,2},{2,3},{4,5},{5,6},{6,7},{8,9},{9,10},{10,11},{12,13},{... | collective-permute-start | bytes 55448 | tf_op jit(solution)/shard_map/ppermute | solution.py:19
  53.1 2.9 %fusion.104 = f32[130,130,32]{1,2,0:T(8,128)} fusion(bf16[2,35,132]{2,1,0:T(8,128)(2,1)S(1)} %collective-permute-done.4, bf16[128,35,132]{2,1,0:T(8,128)(2,1)S(1)} %copy.58, bf16[2,35,132]{2,1,0:T(8,128)(2,1)S(1)} %collective-permute-done.3, bf16[3,3,32,3]{2,3,1,0:T(4,128)(2,1)S(1)} %copy-done.10), kind=kOutput, calls=%fused_computation.133 | convolution fusion | flops 3549000 | bytes 4867584 | tf_op jit(solution)/shard_map/oi,xiy->xoy/dot_general | solution.py:37
  56.0 2.8 %fusion.114 = f32[130,130,32]{1,2,0:T(8,128)} fusion(bf16[2,35,132]{2,1,0:T(8,128)(2,1)S(1)} %collective-permute-done.4, bf16[128,35,132]{2,1,0:T(8,128)(2,1)S(1)} %copy.58, bf16[3,3,32,3]{2,3,1,0:T(4,128)(2,1)S(1)} %copy-done.10), kind=kOutput, calls=%fused_computation.143 | convolution fusion | flops 3447600 | bytes 4826624 | tf_op jit(solution)/shard_map/oi,xiy->xoy/dot_general | solution.py:37
  58.8 2.8 %fusion.118 = f32[130,130,32]{1,2,0:T(8,128)} fusion(bf16[2,35,132]{2,1,0:T(8,128)(2,1)S(1)} %collective-permute-done.4, bf16[128,35,132]{2,1,0:T(8,128)(2,1)S(1)} %copy.58, bf16[2,35,132]{2,1,0:T(8,128)(2,1)S(1)} %collective-permute-done.3, bf16[3,3,32,3]{2,3,1,0:T(4,128)(2,1)S(1)} %copy-done.10), kind=kOutput, calls=%fused_computation.147 | convolution fusion | flops 3549000 | bytes 4867584 | tf_op jit(solution)/shard_map/oi,xiy->xoy/dot_general | solution.py:37
  67.0 2.8 %fusion.138 = f32[130,130,32]{1,2,0:T(8,128)} fusion(bf16[128,35,132]{2,1,0:T(8,128)(2,1)S(1)} %copy.58, bf16[2,35,132]{2,1,0:T(8,128)(2,1)S(1)} %collective-permute-done.3, bf16[3,3,32,3]{2,3,1,0:T(4,128)(2,1)S(1)} %copy-done.10), kind=kOutput, calls=%fused_computation.167 | convolution fusion | flops 3447600 | bytes 4826624 | tf_op jit(solution)/shard_map/oi,xiy->xoy/dot_general | solution.py:37
  69.8 2.8 %fusion.132 = f32[130,130,32]{1,2,0:T(8,128)} fusion(bf16[2,35,132]{2,1,0:T(8,128)(2,1)S(1)} %collective-permute-done.4, bf16[128,35,132]{2,1,0:T(8,128)(2,1)S(1)} %copy.58, bf16[2,35,132]{2,1,0:T(8,128)(2,1)S(1)} %collective-permute-done.3, bf16[3,3,32,3]{2,3,1,0:T(4,128)(2,1)S(1)} %copy-done.10), kind=kOutput, calls=%fused_computation.161 | convolution fusion | flops 3549000 | bytes 4867584 | tf_op jit(solution)/shard_map/oi,xiy->xoy/dot_general | solution.py:37
  72.6 14.8 %fusion.34 = (bf16[130,32,130]{2,1,0:T(8,128)(2,1)S(1)}, f32[130,130,32]{1,2,0:T(8,128)}) fusion(pred[130,130]{1,0:T(8,128)(4,1)S(1)} %broadcast_and_fusion, f32[32]{0:T(128)S(1)} %copy-done.12, bf16[3,3,32,3]{2,3,1,0:T(4,128)(2,1)S(1)} %copy-done.10, bf16[2,35,132]{2,1,0:T(8,128)(2,1)S(1)} %collective-permute-done.4, bf16[128,35,132]{2,1,0:T(8,128)(2,1)S(1)} %copy.58, ...), kind=kOutput, calls=%fused_computation.44 | convolution fusion | flops 11559600 | bytes 23249152 | tf_op jit(solution)/shard_map/oi,xiy->xoy/dot_general | solution.py:37
  105.3 3.1 %fusion.55 = f32[130,130,32]{1,2,0:T(8,128)} fusion(bf16[132,35,132]{2,1,0:T(8,128)(2,1)S(1)} %pad_maximum_fusion.1, bf16[3,3,32,32]{3,2,1,0:T(8,128)(2,1)S(1)} %copy-done.8), kind=kOutput, calls=%fused_computation.73 | convolution fusion | flops 34611200 | bytes 4301312 | tf_op jit(solution)/shard_map/oi,xoy->xiy/dot_general | solution.py:56
  108.5 3.2 %fusion.57 = f32[130,130,32]{1,2,0:T(8,128)} fusion(bf16[132,35,132]{2,1,0:T(8,128)(2,1)S(1)} %pad_maximum_fusion.1, bf16[3,3,32,32]{3,2,1,0:T(8,128)(2,1)S(1)} %copy-done.8), kind=kOutput, calls=%fused_computation.75 | convolution fusion | flops 34611200 | bytes 4301312 | tf_op jit(solution)/shard_map/oi,xoy->xiy/dot_general | solution.py:56
  111.6 2.8 %fusion.53 = f32[130,130,32]{1,2,0:T(8,128)} fusion(bf16[2,35,132]{2,1,0:T(8,128)(2,1)S(1)} %collective-permute-done.4, bf16[128,35,132]{2,1,0:T(8,128)(2,1)S(1)} %copy.58, bf16[3,3,32,32]{3,2,1,0:T(8,128)(2,1)S(1)} %copy-done.8), kind=kOutput, calls=%fused_computation.71 | convolution fusion | flops 36774400 | bytes 4833792 | tf_op jit(solution)/shard_map/oi,xoy->xiy/dot_general | solution.py:56
  114.5 3.6 %fusion.44 = f32[130,130,32]{1,2,0:T(8,128)} fusion(bf16[128,35,132]{2,1,0:T(8,128)(2,1)S(1)} %copy.58, bf16[2,35,132]{2,1,0:T(8,128)(2,1)S(1)} %collective-permute-done.3, bf16[3,3,32,32]{3,2,1,0:T(8,128)(2,1)S(1)} %copy-done.8), kind=kOutput, calls=%fused_computation.62 | convolution fusion | flops 35152000 | bytes 4833792 | tf_op jit(solution)/shard_map/oi,xoy->xiy/dot_general | solution.py:56
  118.1 3.6 %fusion.38 = f32[130,130,32]{1,2,0:T(8,128)} fusion(bf16[128,35,132]{2,1,0:T(8,128)(2,1)S(1)} %copy.58, bf16[2,35,132]{2,1,0:T(8,128)(2,1)S(1)} %collective-permute-done.4, bf16[3,3,32,32]{3,2,1,0:T(8,128)(2,1)S(1)} %copy-done.8), kind=kOutput, calls=%fused_computation.58 | convolution fusion | flops 35152000 | bytes 4833792 | tf_op jit(solution)/shard_map/oi,xoy->xiy/dot_general | solution.py:56
  121.7 3.9 %fusion.47 = f32[130,130,32]{1,2,0:T(8,128)} fusion(bf16[128,35,132]{2,1,0:T(8,128)(2,1)S(1)} %copy.58, bf16[2,35,132]{2,1,0:T(8,128)(2,1)S(1)} %collective-permute-done.3, bf16[3,3,32,32]{3,2,1,0:T(8,128)(2,1)S(1)} %copy-done.8), kind=kOutput, calls=%fused_computation.64 | convolution fusion | flops 35152000 | bytes 4833792 | tf_op jit(solution)/shard_map/oi,xoy->xiy/dot_general | solution.py:56
  125.7 3.7 %fusion.41 = f32[130,130,32]{1,2,0:T(8,128)} fusion(bf16[128,35,132]{2,1,0:T(8,128)(2,1)S(1)} %copy.58, bf16[2,35,132]{2,1,0:T(8,128)(2,1)S(1)} %collective-permute-done.4, bf16[3,3,32,32]{3,2,1,0:T(8,128)(2,1)S(1)} %copy-done.8), kind=kOutput, calls=%fused_computation.60 | convolution fusion | flops 35152000 | bytes 4833792 | tf_op jit(solution)/shard_map/oi,xoy->xiy/dot_general | solution.py:56
  129.4 15.3 %fusion.29 = bf16[130,32,130]{2,1,0:T(8,128)(2,1)} fusion(f32[130,130,32]{1,2,0:T(8,128)} %get-tuple-element.93, f32[130,130,32]{1,2,0:T(8,128)} %fusion.51, f32[130,130,32]{1,2,0:T(8,128)} %fusion.53, f32[130,130,32]{1,2,0:T(8,128)} %fusion.44, f32[130,130,32]{1,2,0:T(8,128)} %fusion.55, f32[130,130,32]{1,2,0:T(8,128)} %fusion.38, ...), kind=kOutput, calls=%fused_computation.36 | convolution fusion | flops 46508800 | bytes 23255808 | tf_op jit(solution)/shard_map/oi,xoy->xiy/dot_general | solution.py:56
  162.3 3.0 %collective-permute-start.5 = (bf16[128,2,128]{2,1,0:T(2,128)(2,1)S(1)}, bf16[128,2,128]{2,1,0:T(2,128)(2,1)S(1)}, u32[]{:S(2)}, u32[]{:S(2)}) collective-permute-start(bf16[128,2,128]{2,1,0:T(2,128)(2,1)S(1)} %bitcast.290), channel_id=1, source_target_pairs={{4,0},{8,4},{12,8},{16,12},{20,16},{24,20},{28,24},{5,1},{9,5},{13... | collective-permute-start | bytes 196616 | tf_op jit(solution)/shard_map/ppermute | solution.py:11
  165.4 4.2 %fusion.62 = bf16[128,32,128]{2,1,0:T(8,128)(2,1)} fusion(f32[128,128,32]{1,2,0:T(8,128)S(1)} %copy-done, f32[128,128,32]{1,2,0:T(8,128)S(1)} %copy-done.1, f32[128,128,32]{1,2,0:T(8,128)S(1)} %copy-done.2, f32[128,128,32]{1,2,0:T(8,128)S(1)} %copy-done.3, f32[128,128,32]{1,2,0:T(8,128)S(1)} %copy-done.4, f32[128,128,32]{1,2,0:T(8,128)S(1)} %copy-done.5, ...), kind=kOutput, calls=%fused_computation.82 | convolution fusion | flops 38797312 | bytes 18883072 | tf_op jit(solution)/shard_map/oi,xiy->xoy/dot_general | solution.py:37
  169.9 7.5 %all_gather.7 = bf16[512,512]{0,1:T(8,128)(2,1)S(1)} all-gather(bf16[128,512]{0,1:T(8,128)(2,1)S(1)} %bitcast.285), channel_id=1, replica_groups=mesh['strip'=8,'col'=4] {'col'}, dimensions={0}, use_global_device_ids=true | all-gather | bytes 655360 | tf_op jit(solution)/shard_map/all_gather | solution.py:160
  (153 shorter events, 70.6 us)
Async XLA Ops:
  9.3 17.3 %copy-start.9 = (s32[1024,4]{0,1:T(4,128)S(1)}, s32[1024,4]{0,1:T(4,128)}, u32[]{:S(2)}) copy-start(s32[1024,4]{0,1:T(4,128)} %param.10) | copy-start | bytes 49156
  9.3 17.3 %copy-start.7 = (bf16[128,32,128]{2,1,0:T(8,128)(2,1)S(1)}, bf16[128,32,128]{2,1,0:T(8,128)(2,1)}, u32[]{:S(2)}) copy-start(bf16[128,32,128]{2,1,0:T(8,128)(2,1)} %param.17) | copy-start | bytes 3145732
  23.3 6.1 %collective-permute-start = (bf16[128,3,128]{0,2,1:T(8,128)(2,1)S(1)}, bf16[128,3,128]{0,2,1:T(8,128)(2,1)S(1)}, u32[]{:S(2)}, u32[]{:S(2)}) collective-permute-start(bf16[128,3,128]{0,2,1:T(8,128)(2,1)S(1)} %fusion.144), channel_id=1, source_target_pairs={{0,4},{4,8},{8,12},{12,16},{16,20},{20,24},{24,28},{1,5},{5,9},{9,... | collective-permute-start | bytes 294920 | tf_op jit(solution)/shard_map/ppermute | solution.py:11
  29.5 6.2 %collective-permute-start.2 = (bf16[128,35,2]{0,2,1:T(2,128)(2,1)S(1)}, bf16[128,35,2]{0,2,1:T(2,128)(2,1)S(1)}, u32[]{:S(2)}, u32[]{:S(2)}) collective-permute-start(bf16[128,35,2]{0,2,1:T(2,128)(2,1)S(1)} %get-tuple-element.87), channel_id=1, source_target_pairs={{4,0},{8,4},{12,8},{16,12},{20,16},{24,20},{28,24},{5,1},{9,5},{13... | collective-permute-start | bytes 53768 | tf_op jit(solution)/shard_map/ppermute | solution.py:22
  32.6 4.5 %collective-permute-start.1 = (bf16[128,35,2]{0,2,1:T(2,128)(2,1)S(1)}, bf16[128,35,2]{0,2,1:T(2,128)(2,1)S(1)}, u32[]{:S(2)}, u32[]{:S(2)}) collective-permute-start(bf16[128,35,2]{0,2,1:T(2,128)(2,1)S(1)} %get-tuple-element.86), channel_id=1, source_target_pairs={{0,4},{4,8},{8,12},{12,16},{16,20},{20,24},{24,28},{1,5},{5,9},{9,... | collective-permute-start | bytes 53768 | tf_op jit(solution)/shard_map/ppermute | solution.py:19
  35.7 14.2 %copy-start.10 = (bf16[3,3,32,3]{2,3,1,0:T(4,128)(2,1)S(1)}, bf16[3,3,32,3]{2,3,1,0:T(4,128)(2,1)}, u32[]{:S(2)}) copy-start(bf16[3,3,32,3]{2,3,1,0:T(4,128)(2,1)} %param.13) | copy-start | bytes 5188
  42.3 7.6 %collective-permute-start.3 = (bf16[2,35,132]{2,1,0:T(8,128)(2,1)S(1)}, bf16[2,35,132]{2,1,0:T(8,128)(2,1)S(1)}, u32[]{:S(2)}, u32[]{:S(2)}) collective-permute-start(bf16[2,35,132]{2,1,0:T(8,128)(2,1)S(1)} %get-tuple-element.84), channel_id=1, source_target_pairs={{0,1},{1,2},{2,3},{4,5},{5,6},{6,7},{8,9},{9,10},{10,11},{12,13},{... | collective-permute-start | bytes 55448 | tf_op jit(solution)/shard_map/ppermute | solution.py:19
  47.8 5.3 %collective-permute-start.4 = (bf16[2,35,132]{2,1,0:T(8,128)(2,1)S(1)}, bf16[2,35,132]{2,1,0:T(8,128)(2,1)S(1)}, u32[]{:S(2)}, u32[]{:S(2)}) collective-permute-start(bf16[2,35,132]{2,1,0:T(8,128)(2,1)S(1)} %get-tuple-element.85), channel_id=1, source_target_pairs={{1,0},{2,1},{3,2},{5,4},{6,5},{7,6},{9,8},{10,9},{11,10},{13,12},{... | collective-permute-start | bytes 55448 | tf_op jit(solution)/shard_map/ppermute | solution.py:22
  69.8 2.8 %copy-start.12 = (f32[32]{0:T(128)S(1)}, f32[32]{0:T(128)}, u32[]{:S(2)}) copy-start(f32[32]{0:T(128)} %param.14) | copy-start | bytes 388
  72.6 14.8 %copy-start.8 = (bf16[3,3,32,32]{3,2,1,0:T(8,128)(2,1)S(1)}, bf16[3,3,32,32]{3,2,1,0:T(8,128)(2,1)}, u32[]{:S(2)}) copy-start(bf16[3,3,32,32]{3,2,1,0:T(8,128)(2,1)} %param.15) | copy-start | bytes 55300
  129.4 36.0 %copy-start.5 = (f32[128,128,32]{1,2,0:T(8,128)S(1)}, f32[128,128,32]{1,2,0:T(8,128)}, u32[]{:S(2)}) copy-start(f32[128,128,32]{1,2,0:T(8,128)} %fusion.89) | copy-start | bytes 6291460
  129.4 36.0 %copy-start.6 = (f32[128,128,32]{1,2,0:T(8,128)S(1)}, f32[128,128,32]{1,2,0:T(8,128)}, u32[]{:S(2)}) copy-start(f32[128,128,32]{1,2,0:T(8,128)} %fusion.93) | copy-start | bytes 6291460
  146.8 18.6 %copy-start.4 = (f32[128,128,32]{1,2,0:T(8,128)S(1)}, f32[128,128,32]{1,2,0:T(8,128)}, u32[]{:S(2)}) copy-start(f32[128,128,32]{1,2,0:T(8,128)} %fusion.87) | copy-start | bytes 6291460
  149.0 16.3 %copy-start.3 = (f32[128,128,32]{1,2,0:T(8,128)S(1)}, f32[128,128,32]{1,2,0:T(8,128)}, u32[]{:S(2)}) copy-start(f32[128,128,32]{1,2,0:T(8,128)} %fusion.85) | copy-start | bytes 6291460
  153.4 12.0 %copy-start.2 = (f32[128,128,32]{1,2,0:T(8,128)S(1)}, f32[128,128,32]{1,2,0:T(8,128)}, u32[]{:S(2)}) copy-start(f32[128,128,32]{1,2,0:T(8,128)} %fusion.83) | copy-start | bytes 6291460
  155.6 9.8 %copy-start = (f32[128,128,32]{1,2,0:T(8,128)S(1)}, f32[128,128,32]{1,2,0:T(8,128)}, u32[]{:S(2)}) copy-start(f32[128,128,32]{1,2,0:T(8,128)} %fusion.79) | copy-start | bytes 6291460
  155.6 9.8 %copy-start.1 = (f32[128,128,32]{1,2,0:T(8,128)S(1)}, f32[128,128,32]{1,2,0:T(8,128)}, u32[]{:S(2)}) copy-start(f32[128,128,32]{1,2,0:T(8,128)} %fusion.81) | copy-start | bytes 6291460
  155.6 9.8 %copy-start.11 = (f32[32]{0:T(128)S(1)}, f32[32]{0:T(128)}, u32[]{:S(2)}) copy-start(f32[32]{0:T(128)} %param.16) | copy-start | bytes 388
  162.3 7.3 %collective-permute-start.5 = (bf16[128,2,128]{2,1,0:T(2,128)(2,1)S(1)}, bf16[128,2,128]{2,1,0:T(2,128)(2,1)S(1)}, u32[]{:S(2)}, u32[]{:S(2)}) collective-permute-start(bf16[128,2,128]{2,1,0:T(2,128)(2,1)S(1)} %bitcast.290), channel_id=1, source_target_pairs={{4,0},{8,4},{12,8},{16,12},{20,16},{24,20},{28,24},{5,1},{9,5},{13... | collective-permute-start | bytes 196616 | tf_op jit(solution)/shard_map/ppermute | solution.py:11
where the time goes:
time: 181 us; the launch traced here: 180 us
  matrix products  124 us (69%)
  starting transfers between devices  19.9 us (11%)
  blocking collectives  13.8 us (8%)
  local copies, waits for them, and re-layouts  9.63 us (5%)
  other arithmetic  7.78 us (4%)
  waiting for transfers between devices  3.59 us (2%)
    dot_general x18, matrix products, conv_back(): jnp.einsum('oi,xoy->xiy', weights[shift_row, shift_col], window, preferre...  59.7 us
    dot_general x18, matrix products, conv_valid(): jnp.einsum('oi,xiy->xoy', weights[shift_row, shift_col], window, preferre...  55.9 us
    ppermute x2, starting transfers between devices, with_halo(): lax.ppermute(lax.slice_in_dim(block, block.shape[dim] - width, None, axis...  8.54 us
    all_gather x1, blocking collectives, shards(): shard_piece = lax.all_gather(both_halves, 'col', axis=0, tiled=True)  7.48 us
    all_gather x1, blocking collectives, shards(): shard_piece = lax.all_gather(packed, 'col', axis=0, tiled=True)  6.3 us
    ppermute x2, starting transfers between devices, from_behind(): return lax.ppermute(x, axis, pairs)  6.19 us
    ppermute x2, starting transfers between devices, with_halo(): lax.ppermute(lax.slice_in_dim(block, 0, width, axis=dim), axis, backward)  5.17 us
    dot_general x4, matrix products, column_block(): jnp.einsum('pk,phr->khr', pin_cols, pin_factor, preferred_element_type=jn...  4.31 us
  transfers between devices with their start and end apart: 6, of which 3 were waited for; matrix products, arithmetic and copies ran while one was open for 4% of the time, Pallas kernels for 0%

commit v1 on v0

--- a/solution.py
+++ b/solution.py
@@ -3,6 +3,22 @@
 import jax.numpy as jnp
 from jax import lax
 from jax.sharding import PartitionSpec as P
+
+
+def ring_gather(x, axis, dim):
+    ways, here, step = (lax.axis_size(axis), lax.axis_index(axis), x.shape[dim])
+    shape = [n * ways if d == dim else n for d, n in enumerate(x.shape)]
+    full = lax.dynamic_update_slice_in_dim(jnp.zeros(shape, x.dtype), x, here * step, axis=dim)
+    going_up = going_down = x
+    for far in range(1, ways // 2 + 1):
+        going_up = lax.ppermute(going_up, axis, [(d, (d + 1) % ways) for d in range(ways)])
+        full = lax.dynamic_update_slice_in_dim(full, going_up, (here - far) % ways * step, axis=dim)
+        if 2 * far < ways:
+            going_down = lax.ppermute(going_down, axis, [(d, (d - 1) % ways) for d in range(ways)])
+            full = lax.dynamic_update_slice_in_dim(
+                full, going_down, (here + far) % ways * step, axis=dim
+            )
+    return full
 
 
 def from_behind(x, axis, by):
@@ -157,7 +173,7 @@
     both_halves = jnp.stack([back_maps, from_below], axis=1).reshape(tile_cols, 4 * span)
     left_col = net_box[:, 0]
     right_col = net_box[:, 1]
-    shard_piece = lax.all_gather(both_halves, "col", axis=0, tiled=True)
+    shard_piece = ring_gather(both_halves, "col", 0)
     piece_cols = jnp.arange(shard_piece.shape[0], dtype=jnp.int32)
     net_cols = (
         (left_col[:, None] <= piece_cols[None, :]) & (piece_cols[None, :] <= right_col[:, None])

time: 181 us -> 177 us (0.978)
  waiting for transfers between devices: 3.59 us -> 13.5 us
  matrix products: 124 us -> 116 us
  blocking collectives: 13.8 us -> 6.3 us
    dot_general x18, matrix products: 59.7 us -> 49.3 us  [conv_back(): jnp.einsum('oi,xoy->xiy', weights[shift_row, shift_col], window, preferre...]
    all_gather x1 -> x0, blocking collectives: 7.48 us -> none  [shards(): shard_piece = lax.all_gather(both_halves, 'col', axis=0, tiled=True)]
    ppermute x2, waiting for transfers between devices: 0.45 us -> 6.56 us  [with_halo(): lax.ppermute(lax.slice_in_dim(block, 0, width, axis=dim), axis, backward)]
    ppermute x0 -> x3, starting transfers between devices: none -> 3 us  [the longest x2 2.99 us: ring_gather(): lax.ppermute(going_up, axis, [(d, (d + 1) % ways) for d in range(ways)])]
    ppermute x0 -> x3, waiting for transfers between devices: none -> 2.89 us  [the longest x1 2.89 us: ring_gather(): lax.ppermute(going_down, axis, [(d, (d - 1) % ways) for d in range(ways)])]
    dot_general x18, matrix products: 55.9 us -> 58.2 us  [conv_valid(): jnp.einsum('oi,xiy->xoy', weights[shift_row, shift_col], window, preferre...]
    ppermute x2, waiting for transfers between devices: 1.8 us -> 4 us  [from_behind(): return lax.ppermute(x, axis, pairs)]
  transfers between devices with their start and end apart: 6 -> 9, of which waited for: 3 -> 5; matrix products, arithmetic and copies ran while one was open for 4% -> 6% of each run, Pallas kernels for 0% -> 0%
where the time goes in v1:
time: 177 us; the launch traced here: 176 us
  matrix products  116 us (66%)
  starting transfers between devices  21.7 us (12%)
  waiting for transfers between devices  13.5 us (8%)
  local copies, waits for them, and re-layouts  9.78 us (6%)
  other arithmetic  7.78 us (4%)
  blocking collectives  6.3 us (4%)
    dot_general x18, matrix products, conv_valid(): jnp.einsum('oi,xiy->xoy', weights[shift_row, shift_col], window, preferre...  58.2 us
    dot_general x18, matrix products, conv_back(): jnp.einsum('oi,xoy->xiy', weights[shift_row, shift_col], window, preferre...  49.3 us
    ppermute x2, starting transfers between devices, with_halo(): lax.ppermute(lax.slice_in_dim(block, block.shape[dim] - width, None, axis...  9.5 us
    ppermute x2, waiting for transfers between devices, with_halo(): lax.ppermute(lax.slice_in_dim(block, 0, width, axis=dim), axis, backward)  6.56 us
    all_gather x1, blocking collectives, shards(): shard_piece = lax.all_gather(packed, 'col', axis=0, tiled=True)  6.3 us
    ppermute x2, starting transfers between devices, from_behind(): return lax.ppermute(x, axis, pairs)  5.23 us
    dot_general x4, matrix products, column_block(): jnp.einsum('pk,phr->khr', pin_cols, pin_factor, preferred_element_type=jn...  4.31 us
    ppermute x2, starting transfers between devices, with_halo(): lax.ppermute(lax.slice_in_dim(block, 0, width, axis=dim), axis, backward)  4.02 us
  transfers between devices with their start and end apart: 9, of which 5 were waited for; matrix products, arithmetic and copies ran while one was open for 6% of the time, Pallas kernels for 0%

profile of v1, /device:TPU:19, one launch (start us, length us, event | category | flops | bytes accessed | tf_op | source)
XLA Modules:
  0.0 176.3 jit_solution(8406529939283590441)
XLA Ops:
  2.9 6.3 %all_gather.3 = f32[4096,13]{0,1:T(8,128)S(1)} all-gather(f32[1024,13]{0,1:T(8,128)S(1)} %pad_maximum_fusion.10), channel_id=1, replica_groups=mesh['strip'=8,'col'=4] {'col'}, dimensions={0}, use_global_device_ids=true | all-gather | bytes 266240 | tf_op jit(solution)/shard_map/all_gather | solution.py:128
  9.4 13.7 %while.11 = (s32[]{:T(128)}, f32[128,2,3,128]{3,0,2,1:T(8,128)S(1)}, f32[4,1024,13]{1,0,2:T(4,128)S(1)}, s32[]{:T(128)}, s32[]{:T(128)}, /*index=5*/s32[]{:T(128)}, s32[]{:T(128)}) while((s32[]{:T(128)}, f32[128,2,3,128]{3,0,2,1:T(8,128)S(1)}, f32[4,1024,13]{1,0,2:T(4,128)S(1)}, s32[]{:T(128)}, s32[]{:T(128)}, ...), condition=%wide.region_1.2_spmd.clone, body=%wide.region_0.1_spmd.clone.sunk | while | flops 408091520 | bytes 3318371 | solution.py:150
  23.3 3.2 %collective-permute-start = (bf16[128,3,128]{0,2,1:T(8,128)(2,1)S(1)}, bf16[128,3,128]{0,2,1:T(8,128)(2,1)S(1)}, u32[]{:S(2)}, u32[]{:S(2)}) collective-permute-start(bf16[128,3,128]{0,2,1:T(8,128)(2,1)S(1)} %fusion.144), channel_id=1, source_target_pairs={{0,4},{4,8},{8,12},{12,16},{16,20},{20,24},{24,28},{1,5},{5,9},{9,... | collective-permute-start | bytes 294920 | tf_op jit(solution)/shard_map/ppermute | solution.py:27
  29.5 4.1 %collective-permute-start.1 = (bf16[128,35,2]{0,2,1:T(2,128)(2,1)S(1)}, bf16[128,35,2]{0,2,1:T(2,128)(2,1)S(1)}, u32[]{:S(2)}, u32[]{:S(2)}) collective-permute-start(bf16[128,35,2]{0,2,1:T(2,128)(2,1)S(1)} %get-tuple-element.86), channel_id=1, source_target_pairs={{0,4},{4,8},{8,12},{12,16},{16,20},{20,24},{24,28},{1,5},{5,9},{9,... | collective-permute-start | bytes 53768 | tf_op jit(solution)/shard_map/ppermute | solution.py:35
  35.5 3.4 %collective-permute-done.2 = bf16[128,35,2]{0,2,1:T(2,128)(2,1)S(1)} collective-permute-done((bf16[128,35,2]{0,2,1:T(2,128)(2,1)S(1)}, bf16[128,35,2]{0,2,1:T(2,128)(2,1)S(1)}, u32[]{:S(2)}, u32[]{:S(2)}) %collective-permute-start.2) | collective-permute-done | bytes 17952 | tf_op jit(solution)/shard_map/ppermute | solution.py:38
  40.6 3.6 %copy.58 = bf16[128,35,132]{2,1,0:T(8,128)(2,1)S(1)} copy(bf16[128,35,132]{0,2,1:T(8,128)(2,1)} %pad_maximum_fusion.8) | data formatting | bytes 2365440 | tf_op jit(solution)/shard_map/concatenate | solution.py:39
  44.2 5.4 %collective-permute-start.3 = (bf16[2,35,132]{2,1,0:T(8,128)(2,1)S(1)}, bf16[2,35,132]{2,1,0:T(8,128)(2,1)S(1)}, u32[]{:S(2)}, u32[]{:S(2)}) collective-permute-start(bf16[2,35,132]{2,1,0:T(8,128)(2,1)S(1)} %get-tuple-element.84), channel_id=1, source_target_pairs={{0,1},{1,2},{2,3},{4,5},{5,6},{6,7},{8,9},{9,10},{10,11},{12,13},{... | collective-permute-start | bytes 55448 | tf_op jit(solution)/shard_map/ppermute | solution.py:35
  51.9 3.1 %collective-permute-done.4 = bf16[2,35,132]{2,1,0:T(8,128)(2,1)S(1)} collective-permute-done((bf16[2,35,132]{2,1,0:T(8,128)(2,1)S(1)}, bf16[2,35,132]{2,1,0:T(8,128)(2,1)S(1)}, u32[]{:S(2)}, u32[]{:S(2)}) %collective-permute-start.4) | collective-permute-done | bytes 18512 | tf_op jit(solution)/shard_map/ppermute | solution.py:38
  58.3 3.2 %fusion.55 = f32[130,130,32]{1,2,0:T(8,128)} fusion(bf16[132,35,132]{2,1,0:T(8,128)(2,1)S(1)} %pad_maximum_fusion.1, bf16[3,3,32,32]{3,2,1,0:T(8,128)(2,1)S(1)} %copy-done.4), kind=kOutput, calls=%fused_computation.73 | convolution fusion | flops 34611200 | bytes 4301312 | tf_op jit(solution)/shard_map/oi,xoy->xiy/dot_general | solution.py:72
  61.5 3.2 %fusion.57 = f32[130,130,32]{1,2,0:T(8,128)} fusion(bf16[132,35,132]{2,1,0:T(8,128)(2,1)S(1)} %pad_maximum_fusion.1, bf16[3,3,32,32]{3,2,1,0:T(8,128)(2,1)S(1)} %copy-done.4), kind=kOutput, calls=%fused_computation.75 | convolution fusion | flops 34611200 | bytes 4301312 | tf_op jit(solution)/shard_map/oi,xoy->xiy/dot_general | solution.py:72
  64.8 2.8 %fusion.132 = f32[130,130,32]{1,2,0:T(8,128)} fusion(bf16[2,35,132]{2,1,0:T(8,128)(2,1)S(1)} %collective-permute-done.4, bf16[128,35,132]{2,1,0:T(8,128)(2,1)S(1)} %copy.58, bf16[2,35,132]{2,1,0:T(8,128)(2,1)S(1)} %collective-permute-done.3, bf16[3,3,32,3]{2,3,1,0:T(4,128)(2,1)S(1)} %copy-done.6), kind=kOutput, calls=%fused_computation.161 | convolution fusion | flops 3549000 | bytes 4867584 | tf_op jit(solution)/shard_map/oi,xiy->xoy/dot_general | solution.py:53
  67.6 2.9 %fusion.118 = f32[130,130,32]{1,2,0:T(8,128)} fusion(bf16[2,35,132]{2,1,0:T(8,128)(2,1)S(1)} %collective-permute-done.4, bf16[128,35,132]{2,1,0:T(8,128)(2,1)S(1)} %copy.58, bf16[2,35,132]{2,1,0:T(8,128)(2,1)S(1)} %collective-permute-done.3, bf16[3,3,32,3]{2,3,1,0:T(4,128)(2,1)S(1)} %copy-done.6), kind=kOutput, calls=%fused_computation.147 | convolution fusion | flops 3549000 | bytes 4867584 | tf_op jit(solution)/shard_map/oi,xiy->xoy/dot_general | solution.py:53
  70.4 2.8 %fusion.114 = f32[130,130,32]{1,2,0:T(8,128)} fusion(bf16[2,35,132]{2,1,0:T(8,128)(2,1)S(1)} %collective-permute-done.4, bf16[128,35,132]{2,1,0:T(8,128)(2,1)S(1)} %copy.58, bf16[3,3,32,3]{2,3,1,0:T(4,128)(2,1)S(1)} %copy-done.6), kind=kOutput, calls=%fused_computation.143 | convolution fusion | flops 3447600 | bytes 4826624 | tf_op jit(solution)/shard_map/oi,xiy->xoy/dot_general | solution.py:53
  76.0 2.9 %fusion.128 = f32[130,130,32]{1,2,0:T(8,128)} fusion(bf16[2,35,132]{2,1,0:T(8,128)(2,1)S(1)} %collective-permute-done.4, bf16[128,35,132]{2,1,0:T(8,128)(2,1)S(1)} %copy.58, bf16[3,3,32,3]{2,3,1,0:T(4,128)(2,1)S(1)} %copy-done.6), kind=kOutput, calls=%fused_computation.157 | convolution fusion | flops 3447600 | bytes 4826624 | tf_op jit(solution)/shard_map/oi,xiy->xoy/dot_general | solution.py:53
  81.6 2.8 %fusion.110 = f32[130,130,32]{1,2,0:T(8,128)} fusion(bf16[128,35,132]{2,1,0:T(8,128)(2,1)S(1)} %copy.58, bf16[2,35,132]{2,1,0:T(8,128)(2,1)S(1)} %collective-permute-done.3, bf16[3,3,32,3]{2,3,1,0:T(4,128)(2,1)S(1)} %copy-done.6), kind=kOutput, calls=%fused_computation.139 | convolution fusion | flops 3447600 | bytes 4826624 | tf_op jit(solution)/shard_map/oi,xiy->xoy/dot_general | solution.py:53
  87.1 12.9 %fusion.34 = (bf16[130,32,130]{2,1,0:T(8,128)(2,1)S(1)}, f32[130,130,32]{1,2,0:T(8,128)S(1)}) fusion(pred[130,130]{1,0:T(8,128)(4,1)S(1)} %broadcast_and_fusion, f32[32]{0:T(128)S(1)} %copy-done.8, bf16[3,3,32,3]{2,3,1,0:T(4,128)(2,1)S(1)} %copy-done.6, bf16[2,35,132]{2,1,0:T(8,128)(2,1)S(1)} %collective-permute-done.4, ...), kind=kOutput, calls=%fused_computation.44 | convolution fusion | flops 11559600 | bytes 23249152 | tf_op jit(solution)/shard_map/oi,xiy->xoy/dot_general | solution.py:53
  113.0 3.7 %fusion.38 = f32[130,130,32]{1,2,0:T(8,128)} fusion(bf16[128,35,132]{2,1,0:T(8,128)(2,1)S(1)} %copy.58, bf16[2,35,132]{2,1,0:T(8,128)(2,1)S(1)} %collective-permute-done.4, bf16[3,3,32,32]{3,2,1,0:T(8,128)(2,1)S(1)} %copy-done.4), kind=kOutput, calls=%fused_computation.58 | convolution fusion | flops 35152000 | bytes 4833792 | tf_op jit(solution)/shard_map/oi,xoy->xiy/dot_general | solution.py:72
  116.7 3.6 %fusion.41 = f32[130,130,32]{1,2,0:T(8,128)} fusion(bf16[128,35,132]{2,1,0:T(8,128)(2,1)S(1)} %copy.58, bf16[2,35,132]{2,1,0:T(8,128)(2,1)S(1)} %collective-permute-done.4, bf16[3,3,32,32]{3,2,1,0:T(8,128)(2,1)S(1)} %copy-done.4), kind=kOutput, calls=%fused_computation.60 | convolution fusion | flops 35152000 | bytes 4833792 | tf_op jit(solution)/shard_map/oi,xoy->xiy/dot_general | solution.py:72
  120.3 3.6 %fusion.44 = f32[130,130,32]{1,2,0:T(8,128)} fusion(bf16[128,35,132]{2,1,0:T(8,128)(2,1)S(1)} %copy.58, bf16[2,35,132]{2,1,0:T(8,128)(2,1)S(1)} %collective-permute-done.3, bf16[3,3,32,32]{3,2,1,0:T(8,128)(2,1)S(1)} %copy-done.4), kind=kOutput, calls=%fused_computation.62 | convolution fusion | flops 35152000 | bytes 4833792 | tf_op jit(solution)/shard_map/oi,xoy->xiy/dot_general | solution.py:72
  123.9 3.7 %fusion.47 = f32[130,130,32]{1,2,0:T(8,128)} fusion(bf16[128,35,132]{2,1,0:T(8,128)(2,1)S(1)} %copy.58, bf16[2,35,132]{2,1,0:T(8,128)(2,1)S(1)} %collective-permute-done.3, bf16[3,3,32,32]{3,2,1,0:T(8,128)(2,1)S(1)} %copy-done.4), kind=kOutput, calls=%fused_computation.64 | convolution fusion | flops 35152000 | bytes 4833792 | tf_op jit(solution)/shard_map/oi,xoy->xiy/dot_general | solution.py:72
  127.6 2.7 %fusion.53 = f32[130,130,32]{1,2,0:T(8,128)} fusion(bf16[2,35,132]{2,1,0:T(8,128)(2,1)S(1)} %collective-permute-done.4, bf16[128,35,132]{2,1,0:T(8,128)(2,1)S(1)} %copy.58, bf16[3,3,32,32]{3,2,1,0:T(8,128)(2,1)S(1)} %copy-done.4), kind=kOutput, calls=%fused_computation.71 | convolution fusion | flops 36774400 | bytes 4833792 | tf_op jit(solution)/shard_map/oi,xoy->xiy/dot_general | solution.py:72
  130.4 14.0 %fusion.29 = bf16[130,32,130]{2,1,0:T(8,128)(2,1)} fusion(f32[130,130,32]{1,2,0:T(8,128)S(1)} %get-tuple-element.93, f32[130,130,32]{1,2,0:T(8,128)} %fusion.51, f32[130,130,32]{1,2,0:T(8,128)} %fusion.53, f32[130,130,32]{1,2,0:T(8,128)} %fusion.44, f32[130,130,32]{1,2,0:T(8,128)} %fusion.55, f32[130,130,32]{1,2,0:T(8,128)} %fusion.38, ...), kind=kOutput, calls=%fused_computation.36 | convolution fusion | flops 46508800 | bytes 25352448 | tf_op jit(solution)/shard_map/oi,xoy->xiy/dot_general | solution.py:72
  160.7 8.2 %fusion.62 = bf16[128,32,128]{2,1,0:T(8,128)(2,1)} fusion(f32[128,128,32]{1,2,0:T(8,128)S(1)} %copy-done.1, f32[128,128,32]{1,2,0:T(8,128)} %fusion.81, f32[128,128,32]{1,2,0:T(8,128)} %fusion.83, f32[128,128,32]{1,2,0:T(8,128)} %fusion.85, f32[128,128,32]{1,2,0:T(8,128)} %fusion.87, f32[128,128,32]{1,2,0:T(8,128)} %fusion.89, f32[128,128,32]{1,2,0:T(8,128)} %fusion.93, ...), kind=kOutput, calls=%fused_computation.82 | convolution fusion | flops 38797312 | bytes 18883072 | tf_op jit(solution)/shard_map/oi,xiy->xoy/dot_general | solution.py:53
  170.8 2.9 %collective-permute-done.7 = bf16[128,512]{0,1:T(8,128)(2,1)S(1)} collective-permute-done((bf16[128,512]{0,1:T(8,128)(2,1)S(1)}, bf16[128,512]{0,1:T(8,128)(2,1)S(1)}, u32[]{:S(2)}, u32[]{:S(2)}) %collective-permute-start.7) | collective-permute-done | bytes 131104 | tf_op jit(solution)/shard_map/ppermute | solution.py:17
  (155 shorter events, 69.5 us)
Async XLA Ops:
  9.3 17.2 %copy-start.5 = (s32[1024,4]{0,1:T(4,128)S(1)}, s32[1024,4]{0,1:T(4,128)}, u32[]{:S(2)}) copy-start(s32[1024,4]{0,1:T(4,128)} %param.10) | copy-start | bytes 49156
  9.3 17.3 %copy-start.3 = (bf16[128,32,128]{2,1,0:T(8,128)(2,1)S(1)}, bf16[128,32,128]{2,1,0:T(8,128)(2,1)}, u32[]{:S(2)}) copy-start(bf16[128,32,128]{2,1,0:T(8,128)(2,1)} %param.17) | copy-start | bytes 3145732
  23.3 6.1 %collective-permute-start = (bf16[128,3,128]{0,2,1:T(8,128)(2,1)S(1)}, bf16[128,3,128]{0,2,1:T(8,128)(2,1)S(1)}, u32[]{:S(2)}, u32[]{:S(2)}) collective-permute-start(bf16[128,3,128]{0,2,1:T(8,128)(2,1)S(1)} %fusion.144), channel_id=1, source_target_pairs={{0,4},{4,8},{8,12},{12,16},{16,20},{20,24},{24,28},{1,5},{5,9},{9,... | collective-permute-start | bytes 294920 | tf_op jit(solution)/shard_map/ppermute | solution.py:27
  29.5 6.0 %collective-permute-start.1 = (bf16[128,35,2]{0,2,1:T(2,128)(2,1)S(1)}, bf16[128,35,2]{0,2,1:T(2,128)(2,1)S(1)}, u32[]{:S(2)}, u32[]{:S(2)}) collective-permute-start(bf16[128,35,2]{0,2,1:T(2,128)(2,1)S(1)} %get-tuple-element.86), channel_id=1, source_target_pairs={{0,4},{4,8},{8,12},{12,16},{16,20},{20,24},{24,28},{1,5},{5,9},{9,... | collective-permute-start | bytes 53768 | tf_op jit(solution)/shard_map/ppermute | solution.py:35
  33.6 5.4 %collective-permute-start.2 = (bf16[128,35,2]{0,2,1:T(2,128)(2,1)S(1)}, bf16[128,35,2]{0,2,1:T(2,128)(2,1)S(1)}, u32[]{:S(2)}, u32[]{:S(2)}) collective-permute-start(bf16[128,35,2]{0,2,1:T(2,128)(2,1)S(1)} %get-tuple-element.87), channel_id=1, source_target_pairs={{4,0},{8,4},{12,8},{16,12},{20,16},{24,20},{28,24},{5,1},{9,5},{13... | collective-permute-start | bytes 53768 | tf_op jit(solution)/shard_map/ppermute | solution.py:38
  44.2 7.6 %collective-permute-start.3 = (bf16[2,35,132]{2,1,0:T(8,128)(2,1)S(1)}, bf16[2,35,132]{2,1,0:T(8,128)(2,1)S(1)}, u32[]{:S(2)}, u32[]{:S(2)}) collective-permute-start(bf16[2,35,132]{2,1,0:T(8,128)(2,1)S(1)} %get-tuple-element.84), channel_id=1, source_target_pairs={{0,1},{1,2},{2,3},{4,5},{5,6},{6,7},{8,9},{9,10},{10,11},{12,13},{... | collective-permute-start | bytes 55448 | tf_op jit(solution)/shard_map/ppermute | solution.py:35
  49.7 5.3 %collective-permute-start.4 = (bf16[2,35,132]{2,1,0:T(8,128)(2,1)S(1)}, bf16[2,35,132]{2,1,0:T(8,128)(2,1)S(1)}, u32[]{:S(2)}, u32[]{:S(2)}) collective-permute-start(bf16[2,35,132]{2,1,0:T(8,128)(2,1)S(1)} %get-tuple-element.85), channel_id=1, source_target_pairs={{1,0},{2,1},{3,2},{5,4},{6,5},{7,6},{9,8},{10,9},{11,10},{13,12},{... | collective-permute-start | bytes 55448 | tf_op jit(solution)/shard_map/ppermute | solution.py:38
  51.8 3.7 %copy-start.4 = (bf16[3,3,32,32]{3,2,1,0:T(8,128)(2,1)S(1)}, bf16[3,3,32,32]{3,2,1,0:T(8,128)(2,1)}, u32[]{:S(2)}) copy-start(bf16[3,3,32,32]{3,2,1,0:T(8,128)(2,1)} %param.15) | copy-start | bytes 55300
  61.5 3.2 %copy-start.6 = (bf16[3,3,32,3]{2,3,1,0:T(4,128)(2,1)S(1)}, bf16[3,3,32,3]{2,3,1,0:T(4,128)(2,1)}, u32[]{:S(2)}) copy-start(bf16[3,3,32,3]{2,3,1,0:T(4,128)(2,1)} %param.13) | copy-start | bytes 5188
  84.3 2.7 %copy-start.8 = (f32[32]{0:T(128)S(1)}, f32[32]{0:T(128)}, u32[]{:S(2)}) copy-start(f32[32]{0:T(128)} %param.14) | copy-start | bytes 388
  100.0 55.2 %copy-start = (bf16[130,32,130]{2,1,0:T(8,128)(2,1)}, bf16[130,32,130]{2,1,0:T(8,128)(2,1)S(1)}, u32[]{:S(2)}) copy-start(bf16[130,32,130]{2,1,0:T(8,128)(2,1)S(1)} %get-tuple-element.92) | copy-start | bytes 3244804
  144.4 6.4 %copy-start.2 = (bf16[130,32,130]{2,1,0:T(8,128)(2,1)S(1)}, bf16[130,32,130]{2,1,0:T(8,128)(2,1)}, u32[]{:S(2)}) copy-start(bf16[130,32,130]{2,1,0:T(8,128)(2,1)} %fusion.29) | copy-start | bytes 3244804
  152.9 7.8 %copy-start.1 = (f32[128,128,32]{1,2,0:T(8,128)S(1)}, f32[128,128,32]{1,2,0:T(8,128)}, u32[]{:S(2)}) copy-start(f32[128,128,32]{1,2,0:T(8,128)} %fusion.79) | copy-start | bytes 6291460
  152.9 7.8 %copy-start.7 = (f32[32]{0:T(128)S(1)}, f32[32]{0:T(128)}, u32[]{:S(2)}) copy-start(f32[32]{0:T(128)} %param.16) | copy-start | bytes 388
  153.1 6.0 %collective-permute-start.5 = (bf16[128,2,128]{2,1,0:T(2,128)(2,1)S(1)}, bf16[128,2,128]{2,1,0:T(2,128)(2,1)S(1)}, u32[]{:S(2)}, u32[]{:S(2)}) collective-permute-start(bf16[128,2,128]{2,1,0:T(2,128)(2,1)S(1)} %bitcast.292), channel_id=1, source_target_pairs={{4,0},{8,4},{12,8},{16,12},{20,16},{24,20},{28,24},{5,1},{9,5},{13... | collective-permute-start | bytes 196616 | tf_op jit(solution)/shard_map/ppermute | solution.py:27
  159.5 9.5 %collective-permute-start.6 = (bf16[128,512]{0,1:T(8,128)(2,1)S(1)}, bf16[128,512]{0,1:T(8,128)(2,1)S(1)}, u32[]{:S(2)}, u32[]{:S(2)}) collective-permute-start(bf16[128,512]{0,1:T(8,128)(2,1)S(1)} %bitcast.285), channel_id=1, source_target_pairs={{0,1},{1,2},{2,3},{3,0},{4,5},{5,6},{6,7},{7,4},{8,9},{9,10},{10,1... | collective-permute-start | bytes 393224 | tf_op jit(solution)/shard_map/ppermute | solution.py:14
  168.9 4.8 %collective-permute-start.7 = (bf16[128,512]{0,1:T(8,128)(2,1)S(1)}, bf16[128,512]{0,1:T(8,128)(2,1)S(1)}, u32[]{:S(2)}, u32[]{:S(2)}) collective-permute-start(bf16[128,512]{0,1:T(8,128)(2,1)S(1)} %bitcast.286), channel_id=1, source_target_pairs={{0,3},{1,0},{2,1},{3,2},{4,7},{5,4},{6,5},{7,6},{8,11},{9,8},{10,9... | collective-permute-start | bytes 393224 | tf_op jit(solution)/shard_map/ppermute | solution.py:17
  169.0 4.8 %collective-permute-start.8 = (bf16[128,512]{0,1:T(8,128)(2,1)S(1)}, bf16[128,512]{0,1:T(8,128)(2,1)S(1)}, u32[]{:S(2)}, u32[]{:S(2)}) collective-permute-start(bf16[128,512]{0,1:T(8,128)(2,1)S(1)} %collective-permute-done.6), channel_id=1, source_target_pairs={{0,1},{1,2},{2,3},{3,0},{4,5},{5,6},{6,7},{7,4},{8,9},{9,10},{10,1... | collective-permute-start | bytes 393224 | tf_op jit(solution)/shard_map/ppermute | solution.py:14
